TPU v7x, 256 devices: a whole 4x4x8 slice. The times are simulated.
256 devices in a mesh: group: 16 (over y, x), member: 16 (over z, core).
Axes of the slice: x: 4, y: 4, z: 8, core: 2. Of those that a mesh axis runs over, the one named last changes fastest.
Arguments:
- queries: bfloat16 [65536, 6144], P(('group', 'member')), may hold values from -64 to 64
- keys_values: bfloat16 [512, 128, 2048], P('group', 'member'), may hold values from -8 to 8
- local_lists: int32 [512, 5], P(('group', 'member')), may hold values from -1 to 31, as said below
- remote_lists: int32 [512, 3], P(('group', 'member')), may hold values from -1 to 15, as said below
- send_blocks: int32 [16, 16], P('group'), may hold values from 0 to 31
Outputs:
- attended: bfloat16 [65536, 6144], P(('group', 'member'))
Inputs may be any that keep to these rules, and one draw needn't show every extreme that they name: `local_lists`: row i lists distinct blocks of its slab, numbered 0 to 31 within the slab, then -1 in the remaining entries; the first entry is i mod 32, the row's own block. Some row lists 5 blocks. `remote_lists`: row i lists distinct slabs other than its own slab i // 32, then -1 in the remaining entries; a row may list none. Some row lists 3 slabs.
All inputs are finite; a program needn't handle non-finite values.
Results may differ from a plain program's by a relative error of at most 0.0038.
Values may be sent and summed in bfloat16 or wider, within the bound.
A program may use at most 128 MiB of HBM per device.

v0:
```python
import jax
import jax.numpy as jnp
from jax import lax
from jax.sharding import PartitionSpec as P

HEADS = 48
KV_HEADS = 8
HEAD_DIM = 128


def attend_rows(query_rows, listed, usable):
    block_rows = query_rows.shape[0]
    key_width = KV_HEADS * HEAD_DIM
    repeat = HEADS // KV_HEADS
    query_heads = query_rows.reshape(block_rows, KV_HEADS, repeat, HEAD_DIM)
    keys_all = listed[:, :, :key_width].reshape(
        listed.shape[0], listed.shape[1], KV_HEADS, HEAD_DIM
    )
    values_all = listed[:, :, key_width:].reshape(
        listed.shape[0], listed.shape[1], KV_HEADS, HEAD_DIM
    )
    halves = 2
    head_span = KV_HEADS // halves
    pieces = []
    for part_index in range(halves):
        start_head = part_index * head_span
        query_part = query_heads[:, start_head : start_head + head_span]
        keys_part = keys_all[:, :, start_head : start_head + head_span]
        values_part = values_all[:, :, start_head : start_head + head_span]
        scores = jnp.einsum(
            "qgrd,pkgd->qgrpk", query_part, keys_part, preferred_element_type=jnp.float32
        )
        scores = scores * HEAD_DIM ** (-0.5)
        scores = jnp.where(usable[:, None], scores, -jnp.inf)
        maxima = jnp.max(scores, axis=(3, 4), keepdims=True)
        weights = jnp.exp(scores - maxima)
        totals = jnp.sum(weights, axis=(3, 4))
        rounded = weights.astype(jnp.bfloat16)
        blended = jnp.einsum(
            "qgrpk,pkgd->qgrd", rounded, values_part, preferred_element_type=jnp.float32
        )
        pieces.append(blended / totals[..., None])
    joined = jnp.concatenate(pieces, axis=1)
    return joined.reshape(block_rows, HEADS * HEAD_DIM).astype(jnp.bfloat16)


def shards(queries, keys_values, local_lists, remote_lists, send_blocks):
    targets = send_blocks[0]
    query_count = local_lists.shape[0]
    block_rows = queries.shape[0] // query_count
    outputs = []
    outgoing = jnp.take(keys_values, targets, axis=0)
    arrived = lax.all_to_all(outgoing, "group", split_axis=0, concat_axis=0, tiled=True)
    group_pool = lax.all_gather(keys_values, "member", axis=1, tiled=True)
    cast_pool = lax.all_gather(arrived, "member", axis=1, tiled=True)
    for query_block in range(query_count):
        local_row = local_lists[query_block]
        remote_row = remote_lists[query_block]
        listed = jnp.concatenate(
            [
                jnp.take(group_pool, jnp.maximum(local_row, 0), axis=0),
                jnp.take(cast_pool, jnp.maximum(remote_row, 0), axis=0),
            ],
            axis=0,
        )
        usable = jnp.concatenate([local_row >= 0, remote_row >= 0])
        query_rows = queries[query_block * block_rows : (query_block + 1) * block_rows]
        outputs.append(attend_rows(query_rows, listed, usable))
    return jnp.concatenate(outputs, axis=0)


def solution(mesh):
    placed = (
        P(("group", "member"), None),
        P("group", "member", None),
        P(("group", "member"), None),
        P(("group", "member"), None),
        P("group", None),
    )
    return jax.shard_map(
        shards, mesh=mesh, in_specs=placed, out_specs=P(("group", "member"), None), check_vma=False
    )
```

profile of v0, /device:TPU:1, one launch (start us, length us, event | category | flops | bytes accessed | tf_op | source)
XLA Modules:
  0.0 306.8 jit_solution(815406715089342255)
XLA Ops:
  6.5 0.0 all-gather.5.cloned.1.call-start
  6.5 0.7 fusion.54
  7.2 0.7 compare_and_fusion.4
  7.9 1.8 gather_fusion
  9.7 0.1 broadcast_select_fusion.4
  9.8 17.9 %all_to_all.5 = bf16[16,8,2048]{2,1,0:T(8,128)(2,1)} all-to-all(bf16[16,8,2048]{2,1,0:T(8,128)(2,1)S(1)} %broadcast_select_fusion.4), channel_id=1, replica_groups=mesh['group'=16,'member'=16] {'group'}, dimensions={0} | all-to-all | bytes 1048576 | tf_op jit(solution)/shard_map/all_to_all | solution.py:53
  27.7 0.0 all-gather.5.cloned.1.call-update
  27.7 0.0 all-gather.3.cloned.1.call-start
  27.8 0.7 all-gather.3.cloned.1.call-update
  28.5 2.1 fusion.63
  30.6 0.0 copy-start.11
  30.6 0.0 copy-start.10
  30.6 1.6 copy.82
  32.2 1.6 copy.89
  33.8 0.0 copy-done.11
  33.8 0.0 copy-done.10
  33.8 0.1 pad_add_fusion
  34.0 50.6 %all-gather.5.cloned.1.call-done = bf16[16,128,2048]{2,1,0:T(8,128)(2,1)} async-done(((bf16[16,8,2048]{2,1,0:T(8,128)(2,1)}), bf16[16,128,2048]{2,1,0:T(8,128)(2,1)}) %all-gather.5.cloned.1.call-update) | async-done | bytes 8388624 | tf_op jit(solution)/shard_map/all_gather | solution.py:55
  84.6 4.0 %gather_fusion.4 = bf16[3,128,2048]{2,1,0:T(8,128)(2,1)S(1)} fusion(bf16[16,128,2048]{2,1,0:T(8,128)(2,1)} %all-gather.5.cloned.1.call-done, s32[1024]{0:T(1024)S(1)} %pad_clamp_fusion), kind=kCustom, calls=%fused_computation.3.clone | custom fusion | bytes 3145740 | tf_op jit(solution)/shard_map/jit(_take)/gather | solution.py:62
  88.6 4.0 %gather_fusion.2 = bf16[3,128,2048]{2,1,0:T(8,128)(2,1)S(1)} fusion(bf16[16,128,2048]{2,1,0:T(8,128)(2,1)} %all-gather.5.cloned.1.call-done, s32[1024]{0:T(1024)S(1)} %pad_clamp_fusion.2), kind=kCustom, calls=%fused_computation.1.clone | custom fusion | bytes 3145740 | tf_op jit(solution)/shard_map/jit(_take)/gather | solution.py:62
  92.7 2.0 broadcast_select_fusion.2
  94.7 85.7 %all-gather.3.cloned.1.call-done = bf16[32,128,2048]{2,1,0:T(8,128)(2,1)} async-done(((bf16[32,8,2048]{2,1,0:T(8,128)(2,1)}), bf16[32,128,2048]{2,1,0:T(8,128)(2,1)}) %all-gather.3.cloned.1.call-update) | async-done | bytes 16777232 | tf_op jit(solution)/shard_map/all_gather | solution.py:54
  180.4 8.1 %gather_fusion.3 = bf16[5,128,2048]{2,1,0:T(8,128)(2,1)} fusion(bf16[32,128,2048]{2,1,0:T(8,128)(2,1)} %all-gather.3.cloned.1.call-done, s32[1024]{0:T(1024)S(1)} %pad_clamp_fusion.1), kind=kCustom, calls=%fused_computation.2.clone | custom fusion | bytes 5242900 | tf_op jit(solution)/shard_map/jit(_take)/gather | solution.py:61
  188.5 8.1 %gather_fusion.1 = bf16[5,128,2048]{2,1,0:T(8,128)(2,1)} fusion(bf16[32,128,2048]{2,1,0:T(8,128)(2,1)} %all-gather.3.cloned.1.call-done, s32[1024]{0:T(1024)S(1)} %pad_clamp_fusion.4), kind=kCustom, calls=%fused_computation.clone | custom fusion | bytes 5242900 | tf_op jit(solution)/shard_map/jit(_take)/gather | solution.py:61
  196.7 3.2 %broadcast_select_fusion = (bf16[5,128,2048]{2,1,0:T(8,128)(2,1)S(1)}, bf16[5,128,2048]{2,1,0:T(8,128)(2,1)S(1)}) fusion(bf16[5,128,2048]{2,1,0:T(8,128)(2,1)} %gather_fusion.3, pred[5]{0:T(512)(128)(4,1)S(1)} %get-tuple-element.37, bf16[5,128,2048]{2,1,0:T(8,128)(2,1)} %gather_fusion.1, pred[5]{0:T(512)(128)(4,1)S(1)} %get-tuple-element.11), kind=kLoop, calls=%fused_computation.42 | loop fusion | flops 2621440 | bytes 10485770 | tf_op jit(solution)/shard_map/jit(_take)/select_n | solution.py:61
  199.8 0.0 copy-done
  199.9 2.3 fusion.24
  202.1 3.9 %copy.43 = bf16[8,128,1024]{1,2,0:T(8,128)(2,1)} copy(bf16[8,128,1024]{2,1,0:T(8,128)(2,1)} %get-tuple-element.21) | data formatting | bytes 4194304 | tf_op jit(solution)/shard_map/slice | solution.py:19
  206.0 3.1 %fusion.66 = (bf16[8,128,4,128]{1,3,2,0:T(8,128)(2,1)}, bf16[8,128,4,128]{1,3,2,0:T(8,128)(2,1)}) fusion(bf16[8,128,8,128]{1,3,2,0:T(8,128)(2,1)} %bitcast.206), kind=kLoop, calls=%fused_computation.115 | loop fusion | bytes 4194304 | tf_op jit(solution)/shard_map/slice | solution.py:29
  209.1 3.9 %copy.45 = bf16[8,128,1024]{1,2,0:T(8,128)(2,1)} copy(bf16[8,128,1024]{2,1,0:T(8,128)(2,1)} %get-tuple-element.22) | data formatting | bytes 4194304 | tf_op jit(solution)/shard_map/slice | solution.py:16
  213.0 3.1 %fusion.67 = (bf16[8,128,4,128]{1,3,2,0:T(8,128)(2,1)}, bf16[8,128,4,128]{1,3,2,0:T(8,128)(2,1)}) fusion(bf16[8,128,8,128]{1,3,2,0:T(8,128)(2,1)} %bitcast.207), kind=kLoop, calls=%fused_computation.116 | loop fusion | bytes 4194304 | tf_op jit(solution)/shard_map/slice | solution.py:28
  216.2 2.3 copy.88
  218.4 2.3 copy.92
  220.7 3.4 %fusion.25 = (bf16[8,128,1024]{2,1,0:T(8,128)(2,1)}, bf16[8,128,1024]{2,1,0:T(8,128)(2,1)}) fusion(bf16[5,128,2048]{2,1,0:T(8,128)(2,1)S(1)} %get-tuple-element.48, bf16[3,128,2048]{2,1,0:T(8,128)(2,1)} %get-tuple-element.50), kind=kLoop, calls=%fused_computation.45 | loop fusion | flops 8388608 | bytes 8388608 | tf_op jit(solution)/shard_map/concatenate | solution.py:59
  224.2 3.0 copy.32
  227.2 1.5 fusion.64
  228.7 3.0 copy.34
  231.7 0.0 copy-start.1
  231.7 1.5 fusion.65
  233.2 2.4 copy.81
  235.6 2.3 copy.85
  237.9 0.0 copy-done.1
  237.9 0.0 copy-done.3
  237.9 6.3 %bitcast_reduce_fusion.1 = (f32[128,4,6]{0,2,1:T(8,128)S(1)}, f32[4,8,128,128,6]{3,2,4,1,0:T(8,128)}) fusion(pred[8]{0:T(512)(128)(4,1)S(1)} %get-tuple-element.52, bf16[128,8,6,128]{0,3,2,1:T(8,128)(2,1)S(1)} %bitcast.214, bf16[8,128,4,128]{3,1,0,2:T(8,128)(2,1)S(1)} %copy-done.1), kind=kOutput, calls=%fused_computation.9 | convolution fusion | flops 814740480 | bytes 14430720 | tf_op jit(solution)/shard_map/qgrd,pkgd->qgrpk/dot_general | solution.py:30
  244.2 0.0 copy-done.5
  244.2 7.5 %fusion.8 = (f32[128,4,6]{0,2,1:T(8,128)S(1)}, f32[128,4,6]{0,2,1:T(8,128)S(1)}, f32[4,8,128,128,6]{3,2,4,1,0:T(8,128)S(1)}) fusion(f32[4,8,128,128,6]{3,2,4,1,0:T(8,128)} %get-tuple-element.42, f32[128,4,6]{0,2,1:T(8,128)S(1)} %get-tuple-element.41, pred[8]{0:T(512)(128)(4,1)S(1)} %get-tuple-element.52, bf16[128,8,6,128]{0,3,2,1:T(8,128)(2,1)S(1)} %bitcast.215, ...), kind=kOutput, calls=%fused_computation.25 | convolution fusion | flops 827320320 | bytes 27042304 | tf_op jit(solution)/shard_map/qgrd,pkgd->qgrpk/dot_general | solution.py:30
  251.7 0.0 copy-done.9
  251.7 7.6 %fusion.27 = bf16[128,4,6,128]{0,3,2,1:T(8,128)(2,1)S(1)} fusion(f32[4,8,128,128,6]{3,2,4,1,0:T(8,128)} %get-tuple-element.42, f32[128,4,6]{0,2,1:T(8,128)S(1)} %get-tuple-element.41, pred[8]{0:T(512)(128)(4,1)S(1)} %get-tuple-element.52, bf16[8,128,4,128]{1,3,2,0:T(8,128)(2,1)S(1)} %copy-done.9, f32[128,4,6]{0,2,1:T(8,128)S(1)} %get-tuple-element.9), kind=kOutput, calls=%fused_computation.51 | convolution fusion | flops 818675712 | bytes 14442504 | tf_op jit(solution)/shard_map/qgrpk,pkgd->qgrd/dot_general | solution.py:39
  259.3 0.0 copy-start.7
  259.3 2.5 fusion.10
  261.8 0.0 copy-done.7
  261.9 3.3 %fusion.26 = bf16[128,4,6,128]{0,3,2,1:T(8,128)(2,1)S(1)} fusion(f32[4,8,128,128,6]{3,2,4,1,0:T(8,128)S(1)} %get-tuple-element.43, f32[128,4,6]{0,2,1:T(8,128)S(1)} %get-tuple-element.10, pred[8]{0:T(512)(128)(4,1)S(1)} %get-tuple-element.52, bf16[8,128,4,128]{1,3,2,0:T(8,128)(2,1)S(1)} %copy-done.7, f32[128,4,6]{0,2,1:T(8,128)S(1)} %fusion.10), kind=kOutput, calls=%fused_computation.49 | convolution fusion | flops 818675712 | bytes 14442504 | tf_op jit(solution)/shard_map/qgrpk,pkgd->qgrd/dot_general | solution.py:39
  265.1 0.1 pad_maximum_fusion.4
  265.3 0.7 copy.55
  266.0 0.0 copy-start.4
  266.0 7.9 %bitcast_reduce_fusion.3 = (f32[128,4,6]{0,2,1:T(8,128)S(1)}, f32[4,8,128,128,6]{3,2,4,1,0:T(8,128)}) fusion(pred[8]{0:T(512)(128)(4,1)S(1)} %get-tuple-element.51, bf16[128,8,6,128]{0,3,2,1:T(8,128)(2,1)} %bitcast.212, bf16[8,128,4,128]{3,1,0,2:T(8,128)(2,1)} %copy.81), kind=kOutput, calls=%fused_computation.15 | convolution fusion | flops 814740480 | bytes 14430216 | tf_op jit(solution)/shard_map/qgrd,pkgd->qgrpk/dot_general | solution.py:30
  273.9 7.5 %fusion.4 = (f32[128,4,6]{0,2,1:T(8,128)S(1)}, f32[128,4,6]{0,2,1:T(8,128)S(1)}, f32[4,8,128,128,6]{3,2,4,1,0:T(8,128)S(1)}) fusion(f32[4,8,128,128,6]{3,2,4,1,0:T(8,128)} %get-tuple-element.45, f32[128,4,6]{0,2,1:T(8,128)S(1)} %get-tuple-element.44, pred[8]{0:T(512)(128)(4,1)S(1)} %get-tuple-element.51, bf16[128,8,6,128]{0,3,2,1:T(8,128)(2,1)S(1)} %bitcast.213, ...), kind=kOutput, calls=%fused_computation.21 | convolution fusion | flops 827320320 | bytes 27042304 | tf_op jit(solution)/shard_map/qgrd,pkgd->qgrpk/dot_general | solution.py:30
  281.4 7.6 %fusion.29 = bf16[128,4,6,128]{0,3,2,1:T(8,128)(2,1)S(1)} fusion(f32[4,8,128,128,6]{3,2,4,1,0:T(8,128)} %get-tuple-element.45, f32[128,4,6]{0,2,1:T(8,128)S(1)} %get-tuple-element.44, pred[8]{0:T(512)(128)(4,1)S(1)} %get-tuple-element.51, bf16[8,128,4,128]{1,3,2,0:T(8,128)(2,1)S(1)} %copy-done.8, f32[128,4,6]{0,2,1:T(8,128)S(1)} %get-tuple-element.6), kind=kOutput, calls=%fused_computation.55 | convolution fusion | flops 818675712 | bytes 14442504 | tf_op jit(solution)/shard_map/qgrpk,pkgd->qgrd/dot_general | solution.py:39
  289.1 0.0 copy-start.6
  289.1 2.5 fusion.6
  291.6 3.3 %fusion.28 = bf16[128,4,6,128]{0,3,2,1:T(8,128)(2,1)S(1)} fusion(f32[4,8,128,128,6]{3,2,4,1,0:T(8,128)S(1)} %get-tuple-element.46, f32[128,4,6]{0,2,1:T(8,128)S(1)} %get-tuple-element.8, pred[8]{0:T(512)(128)(4,1)S(1)} %get-tuple-element.51, bf16[8,128,4,128]{1,3,2,0:T(8,128)(2,1)S(1)} %copy-done.6, f32[128,4,6]{0,2,1:T(8,128)S(1)} %fusion.6), kind=kOutput, calls=%fused_computation.53 | convolution fusion | flops 818675712 | bytes 14442504 | tf_op jit(solution)/shard_map/qgrpk,pkgd->qgrd/dot_general | solution.py:39
  294.9 0.1 pad_maximum_fusion.3
  295.0 1.6 copy.54
  296.6 3.3 %pad_maximum_fusion = bf16[256,6144]{1,0:T(8,128)(2,1)} fusion(bf16[128,6144]{1,0:T(8,128)(2,1)S(1)} %copy.55, bf16[128,6144]{1,0:T(8,128)(2,1)} %copy.54), kind=kLoop, calls=%fused_computation.41 | loop fusion | flops 6291456 | bytes 6291456 | tf_op jit(solution)/shard_map/concatenate | solution.py:69
  (19 shorter events, 0.1 us)
Async XLA Ops:
  6.5 78.1 %all-gather.5.cloned.1.call-start = ((), (), s32[]{:S(2)}) async-start(), calls=%async_computation.2 | async-start | bytes 8912896 | tf_op jit(solution)/shard_map/all_gather | solution.py:55
  27.7 152.7 %all-gather.3.cloned.1.call-start = ((), (), s32[]{:S(2)}) async-start(), calls=%async_computation.1 | async-start | bytes 17825792 | tf_op jit(solution)/shard_map/all_gather | solution.py:54
  30.6 3.2 %copy-start.11 = (s32[2,5]{1,0:T(2,128)S(1)}, s32[2,5]{1,0:T(2,128)}, u32[]{:S(2)}) copy-start(s32[2,5]{1,0:T(2,128)} %param.11) | copy-start | bytes 124
  30.6 3.2 %copy-start.10 = (s32[2,3]{1,0:T(2,128)S(1)}, s32[2,3]{1,0:T(2,128)}, u32[]{:S(2)}) copy-start(s32[2,3]{1,0:T(2,128)} %param.12) | copy-start | bytes 76
  196.7 3.2 %copy-start = (bf16[3,128,2048]{2,1,0:T(8,128)(2,1)S(1)}, bf16[3,128,2048]{2,1,0:T(8,128)(2,1)}, u32[]{:S(2)}) copy-start(bf16[3,128,2048]{2,1,0:T(8,128)(2,1)} %get-tuple-element.49) | copy-start | bytes 4718596
  231.7 6.2 %copy-start.1 = (bf16[8,128,4,128]{3,1,0,2:T(8,128)(2,1)S(1)}, bf16[8,128,4,128]{3,1,0,2:T(8,128)(2,1)}, u32[]{:S(2)}) copy-start(bf16[8,128,4,128]{3,1,0,2:T(8,128)(2,1)} %copy.88) | copy-start | bytes 3145732
  233.2 4.7 %copy-start.3 = (bf16[128,6144]{0,1:T(8,128)(2,1)S(1)}, bf16[128,6144]{0,1:T(8,128)(2,1)}, u32[]{:S(2)}) copy-start(bf16[128,6144]{0,1:T(8,128)(2,1)} %copy.89) | copy-start | bytes 4718596
  237.9 6.3 %copy-start.5 = (bf16[8,128,4,128]{3,1,0,2:T(8,128)(2,1)S(1)}, bf16[8,128,4,128]{3,1,0,2:T(8,128)(2,1)}, u32[]{:S(2)}) copy-start(bf16[8,128,4,128]{3,1,0,2:T(8,128)(2,1)} %copy.92) | copy-start | bytes 3145732
  244.2 7.5 %copy-start.9 = (bf16[8,128,4,128]{1,3,2,0:T(8,128)(2,1)S(1)}, bf16[8,128,4,128]{1,3,2,0:T(8,128)(2,1)}, u32[]{:S(2)}) copy-start(bf16[8,128,4,128]{1,3,2,0:T(8,128)(2,1)} %get-tuple-element.29) | copy-start | bytes 3145732
  259.3 2.5 copy-start.7
  266.0 7.9 %copy-start.2 = (bf16[128,6144]{0,1:T(8,128)(2,1)S(1)}, bf16[128,6144]{0,1:T(8,128)(2,1)}, u32[]{:S(2)}) copy-start(bf16[128,6144]{0,1:T(8,128)(2,1)} %copy.82) | copy-start | bytes 4718596
  266.0 7.9 %copy-start.4 = (bf16[8,128,4,128]{3,1,0,2:T(8,128)(2,1)S(1)}, bf16[8,128,4,128]{3,1,0,2:T(8,128)(2,1)}, u32[]{:S(2)}) copy-start(bf16[8,128,4,128]{3,1,0,2:T(8,128)(2,1)} %copy.85) | copy-start | bytes 3145732
  273.9 7.5 %copy-start.8 = (bf16[8,128,4,128]{1,3,2,0:T(8,128)(2,1)S(1)}, bf16[8,128,4,128]{1,3,2,0:T(8,128)(2,1)}, u32[]{:S(2)}) copy-start(bf16[8,128,4,128]{1,3,2,0:T(8,128)(2,1)} %get-tuple-element.25) | copy-start | bytes 3145732
  289.1 2.5 copy-start.6
Sparse Core Ops, SparseCore 0:
  27.8 56.7 all-gather.4
  86.5 93.9 all-gather.2
where the time goes:
time: 308 us; the launch traced here: 307 us
  waiting for transfers between devices  137 us (44%)
  local copies, waits for them, and re-layouts  66 us (21%)
  matrix products  51 us (17%)
  other arithmetic  21.1 us (7%)
  blocking collectives  17.9 us (6%)
  between operations  13.7 us (4%)
    all_gather x1, waiting for transfers between devices, shards(): group_pool = lax.all_gather(keys_values, 'member', axis=1, tiled=True)  85.7 us
    all_gather x1, waiting for transfers between devices, shards(): cast_pool = lax.all_gather(arrived, 'member', axis=1, tiled=True)  50.6 us
    dot_general x4, matrix products, attend_rows(): jnp.einsum('qgrd,pkgd->qgrpk', query_part, keys_part, preferred_element_t...  29.2 us
    dot_general x4, matrix products, attend_rows(): jnp.einsum('qgrpk,pkgd->qgrd', rounded, values_part, preferred_element_ty...  21.8 us
    all_to_all x1, blocking collectives, shards(): lax.all_to_all(outgoing, 'group', split_axis=0, concat_axis=0, tiled=True)  17.9 us
    gather x2, local copies, waits for them, and re-layouts, shards(): jnp.take(group_pool, jnp.maximum(local_row, 0), axis=0)  16.3 us
    unnamed x30, local copies, waits for them, and re-layouts  12.5 us
    gather x2, local copies, waits for them, and re-layouts, shards(): jnp.take(cast_pool, jnp.maximum(remote_row, 0), axis=0)  8.06 us
  transfers between devices with their start and end apart: 2, of which 2 were waited for; matrix products, arithmetic and copies ran while one was open for 5% of the time, Pallas kernels for 0%

commit v1 on v0

--- a/solution.py
+++ b/solution.py
@@ -51,7 +51,10 @@
     outputs = []
     outgoing = jnp.take(keys_values, targets, axis=0)
     arrived = lax.all_to_all(outgoing, "group", split_axis=0, concat_axis=0, tiled=True)
-    group_pool = lax.all_gather(keys_values, "member", axis=1, tiled=True)
+    devices = lax.axis_size("member")
+    parts = jnp.stack([keys_values for _ in range(devices)])
+    parts = lax.all_to_all(parts, "member", split_axis=0, concat_axis=0)
+    group_pool = jnp.concatenate(parts, axis=1)
     cast_pool = lax.all_gather(arrived, "member", axis=1, tiled=True)
     for query_block in range(query_count):
         local_row = local_lists[query_block]

time: 308 us -> 590 us (1.92)
  waiting for transfers between devices: 137 us -> 387 us
  local copies, waits for them, and re-layouts: 66 us -> 88.3 us
  starting transfers between devices: 0.04 us -> 10.6 us
    all_to_all x0 -> x1, waiting for transfers between devices: none -> 179 us  [shards(): parts = lax.all_to_all(parts, 'member', split_axis=0, concat_axis=0)]
    all_gather x1, waiting for transfers between devices: 50.6 us -> 207 us  [shards(): cast_pool = lax.all_gather(arrived, 'member', axis=1, tiled=True)]
    all_gather x1 -> x0, waiting for transfers between devices: 85.7 us -> none  [shards(): group_pool = lax.all_gather(keys_values, 'member', axis=1, tiled=True)]
    all_to_all x0 -> x1, local copies, waits for them, and re-layouts: none -> 14.1 us  [shards(): parts = lax.all_to_all(parts, 'member', split_axis=0, concat_axis=0)]
    all_to_all x0 -> x1, starting transfers between devices: none -> 10.5 us  [shards(): parts = lax.all_to_all(parts, 'member', split_axis=0, concat_axis=0)]
    another operation x0 -> x1, local copies, waits for them, and re-layouts: none -> 6.89 us  [shards(): parts = jnp.stack([keys_values for _ in range(devices)])]
    unnamed x30 -> x28, local copies, waits for them, and re-layouts: 12.5 us -> 12.4 us
  transfers between devices with their start and end apart: 2 -> 2, of which waited for: 2 -> 2; matrix products, arithmetic and copies ran while one was open for 5% -> 3% of each run, Pallas kernels for 0% -> 0%
where the time goes in v1:
time: 590 us; the launch traced here: 588 us
  waiting for transfers between devices  387 us (66%)
  local copies, waits for them, and re-layouts  88.3 us (15%)
  matrix products  48.9 us (8%)
  other arithmetic  22.2 us (4%)
  blocking collectives  17.9 us (3%)
  between operations  13.7 us (2%)
  starting transfers between devices  10.6 us (2%)
    all_gather x1, waiting for transfers between devices, shards(): cast_pool = lax.all_gather(arrived, 'member', axis=1, tiled=True)  207 us
    all_to_all x1, waiting for transfers between devices, shards(): parts = lax.all_to_all(parts, 'member', split_axis=0, concat_axis=0)  179 us
    dot_general x4, matrix products, attend_rows(): jnp.einsum('qgrd,pkgd->qgrpk', query_part, keys_part, preferred_element_t...  27.2 us
    dot_general x4, matrix products, attend_rows(): jnp.einsum('qgrpk,pkgd->qgrd', rounded, values_part, preferred_element_ty...  21.7 us
    all_to_all x1, blocking collectives, shards(): lax.all_to_all(outgoing, 'group', split_axis=0, concat_axis=0, tiled=True)  17.9 us
    gather x2, local copies, waits for them, and re-layouts, shards(): jnp.take(group_pool, jnp.maximum(local_row, 0), axis=0)  16.3 us
    all_to_all x1, local copies, waits for them, and re-layouts, shards(): parts = lax.all_to_all(parts, 'member', split_axis=0, concat_axis=0)  14.1 us
    unnamed x28, local copies, waits for them, and re-layouts  12.4 us
  transfers between devices with their start and end apart: 2, of which 2 were waited for; matrix products, arithmetic and copies ran while one was open for 3% of the time, Pallas kernels for 0%

profile of v1, /device:TPU:1, one launch (start us, length us, event | category | flops | bytes accessed | tf_op | source)
XLA Modules:
  0.0 588.4 jit_solution(4845622094830279754)
XLA Ops:
  6.5 0.7 fusion.54
  7.2 0.7 compare_and_fusion.4
  7.9 1.8 gather_fusion
  9.7 0.1 broadcast_select_fusion.4
  9.8 17.9 %all_to_all.10 = bf16[16,8,2048]{2,1,0:T(8,128)(2,1)} all-to-all(bf16[16,8,2048]{2,1,0:T(8,128)(2,1)S(1)} %broadcast_select_fusion.4), channel_id=1, replica_groups=mesh['group'=16,'member'=16] {'group'}, dimensions={0} | all-to-all | bytes 1048576 | tf_op jit(solution)/shard_map/all_to_all | solution.py:53
  27.7 6.9 %stack.2 = bf16[16,32,8,2048]{3,2,1,0:T(8,128)(2,1)} broadcast(bf16[32,8,2048]{2,1,0:T(8,128)(2,1)} %param.10), dimensions={1,2,3} | broadcast | bytes 17825792 | tf_op jit(solution)/shard_map/stack | solution.py:55
  34.6 10.5 %all-to-all-start = ((bf16[16,32,8,2048]{3,2,1,0:T(8,128)(2,1)}), bf16[16,32,8,2048]{3,2,1,0:T(8,128)(2,1)}, u32[]{:S(2)}, u32[]{:S(2)}) async-start(bf16[16,32,8,2048]{3,2,1,0:T(8,128)(2,1)} %stack.2), calls=%async_computation | async-start | bytes 33554432 | tf_op jit(solution)/shard_map/all_to_all | solution.py:56
  45.1 0.0 all-gather.2.cloned.1.call-start
  45.2 0.7 all-gather.2.cloned.1.call-update
  45.9 2.1 fusion.63
  48.0 0.0 copy-start.9
  48.0 0.0 copy-start.10
  48.0 1.6 copy.87
  49.5 1.6 copy.94
  51.1 0.0 copy-done.9
  51.1 0.0 copy-done.10
  51.2 0.1 pad_add_fusion
  51.3 206.9 %all-gather.2.cloned.1.call-done = bf16[16,128,2048]{2,1,0:T(8,128)(2,1)} async-done(((bf16[16,8,2048]{2,1,0:T(8,128)(2,1)}), bf16[16,128,2048]{2,1,0:T(8,128)(2,1)}) %all-gather.2.cloned.1.call-update) | async-done | bytes 8388624 | tf_op jit(solution)/shard_map/all_gather | solution.py:58
  258.2 4.0 gather_fusion.2
  262.3 4.0 gather_fusion.4
  266.3 2.0 broadcast_select_fusion.2
  268.3 179.3 %all-to-all-done = bf16[16,32,8,2048]{3,2,1,0:T(8,128)(2,1)} async-done(((bf16[16,32,8,2048]{3,2,1,0:T(8,128)(2,1)}), bf16[16,32,8,2048]{3,2,1,0:T(8,128)(2,1)}, u32[]{:S(2)}, u32[]{:S(2)}) %all-to-all-start) | async-done | bytes 16777248 | tf_op jit(solution)/shard_map/all_to_all | solution.py:56
  447.6 14.1 %copy.116 = bf16[16,32,8,2048]{3,2,0,1:T(8,128)(2,1)} copy(bf16[16,32,8,2048]{3,2,1,0:T(8,128)(2,1)} %all-to-all-done) | data formatting | bytes 33554432 | tf_op jit(solution)/shard_map/all_to_all | solution.py:56
  461.7 8.2 %gather_fusion.1 = bf16[5,128,2048]{2,1,0:T(8,128)(2,1)} fusion(bf16[32,128,2048]{2,1,0:T(8,128)(2,1)} %bitcast.211, s32[1024]{0:T(1024)S(1)} %pad_clamp_fusion.4), kind=kCustom, calls=%fused_computation.clone | custom fusion | bytes 5242900 | tf_op jit(solution)/shard_map/jit(_take)/gather | solution.py:64
  469.8 8.1 %gather_fusion.3 = bf16[5,128,2048]{2,1,0:T(8,128)(2,1)} fusion(bf16[32,128,2048]{2,1,0:T(8,128)(2,1)} %bitcast.212, s32[1024]{0:T(1024)S(1)} %pad_clamp_fusion.1), kind=kCustom, calls=%fused_computation.2.clone | custom fusion | bytes 5242900 | tf_op jit(solution)/shard_map/jit(_take)/gather | solution.py:64
  478.0 3.2 broadcast_select_fusion
  481.1 0.0 copy-done.1
  481.1 2.3 fusion.25
  483.4 3.9 copy.39
  487.3 3.1 fusion.65
  490.4 2.3 copy.86
  492.7 2.3 copy.90
  495.0 3.9 copy.37
  498.9 2.9 fusion.64
  501.8 0.0 copy-done.2
  501.8 0.0 copy-done.4
  501.8 6.3 %bitcast_reduce_fusion.3 = (f32[128,4,6]{0,2,1:T(8,128)S(1)}, f32[4,8,128,128,6]{3,2,4,1,0:T(8,128)}) fusion(pred[8]{0:T(512)(128)(4,1)S(1)} %get-tuple-element.51, bf16[128,8,6,128]{0,3,2,1:T(8,128)(2,1)S(1)} %bitcast.221, bf16[8,128,4,128]{3,1,0,2:T(8,128)(2,1)S(1)} %copy-done.2), kind=kOutput, calls=%fused_computation.16 | convolution fusion | flops 814740480 | bytes 14430720 | tf_op jit(solution)/shard_map/qgrd,pkgd->qgrpk/dot_general | solution.py:30
  508.2 0.0 copy-done.6
  508.2 7.4 %fusion.4 = (f32[128,4,6]{0,2,1:T(8,128)S(1)}, f32[128,4,6]{0,2,1:T(8,128)S(1)}, f32[4,8,128,128,6]{3,2,4,1,0:T(8,128)S(1)}) fusion(f32[4,8,128,128,6]{3,2,4,1,0:T(8,128)} %get-tuple-element.45, f32[128,4,6]{0,2,1:T(8,128)S(1)} %get-tuple-element.44, pred[8]{0:T(512)(128)(4,1)S(1)} %get-tuple-element.51, bf16[128,8,6,128]{0,3,2,1:T(8,128)(2,1)S(1)} %bitcast.222, ...), kind=kOutput, calls=%fused_computation.22 | convolution fusion | flops 827320320 | bytes 27042304 | tf_op jit(solution)/shard_map/qgrd,pkgd->qgrpk/dot_general | solution.py:30
  515.5 7.6 %fusion.29 = bf16[128,4,6,128]{0,3,2,1:T(8,128)(2,1)S(1)} fusion(f32[4,8,128,128,6]{3,2,4,1,0:T(8,128)} %get-tuple-element.45, f32[128,4,6]{0,2,1:T(8,128)S(1)} %get-tuple-element.44, pred[8]{0:T(512)(128)(4,1)S(1)} %get-tuple-element.51, bf16[8,128,4,128]{1,3,2,0:T(8,128)(2,1)S(1)} %get-tuple-element.25, f32[128,4,6]{0,2,1:T(8,128)S(1)} %get-tuple-element.6), kind=kOutput, calls=%fused_computation.56 | convolution fusion | flops 818675712 | bytes 14442504 | tf_op jit(solution)/shard_map/qgrpk,pkgd->qgrd/dot_general | solution.py:39
  523.1 0.0 copy-start.8
  523.1 2.5 fusion.6
  525.7 0.0 copy-done.8
  525.7 3.3 fusion.28
  528.9 1.3 pad_maximum_fusion.3
  530.2 2.6 copy.59
  532.8 3.4 fusion.24
  536.3 3.0 copy.50
  539.3 1.5 fusion.67
  540.8 1.6 copy.93
  542.5 2.3 copy.97
  544.8 3.0 copy.48
  547.8 0.0 copy-start.3
  547.8 1.1 fusion.66
  548.9 0.7 copy-done.3
  549.6 6.3 %bitcast_reduce_fusion.1 = (f32[128,4,6]{0,2,1:T(8,128)S(1)}, f32[4,8,128,128,6]{3,2,4,1,0:T(8,128)}) fusion(pred[8]{0:T(512)(128)(4,1)S(1)} %get-tuple-element.52, bf16[128,8,6,128]{0,3,2,1:T(8,128)(2,1)S(1)} %bitcast.219, bf16[8,128,4,128]{3,1,0,2:T(8,128)(2,1)S(1)} %copy.93), kind=kOutput, calls=%fused_computation.10 | convolution fusion | flops 814740480 | bytes 14430720 | tf_op jit(solution)/shard_map/qgrd,pkgd->qgrpk/dot_general | solution.py:30
  555.9 7.2 %fusion.8 = (f32[128,4,6]{0,2,1:T(8,128)S(1)}, f32[128,4,6]{0,2,1:T(8,128)S(1)}, f32[4,8,128,128,6]{3,2,4,1,0:T(8,128)S(1)}) fusion(f32[4,8,128,128,6]{3,2,4,1,0:T(8,128)} %get-tuple-element.42, f32[128,4,6]{0,2,1:T(8,128)S(1)} %get-tuple-element.41, pred[8]{0:T(512)(128)(4,1)S(1)} %get-tuple-element.52, bf16[128,8,6,128]{0,3,2,1:T(8,128)(2,1)S(1)} %bitcast.220, ...), kind=kOutput, calls=%fused_computation.26 | convolution fusion | flops 827320320 | bytes 27042304 | tf_op jit(solution)/shard_map/qgrd,pkgd->qgrpk/dot_general | solution.py:30
  563.1 7.6 %fusion.27 = bf16[128,4,6,128]{0,3,2,1:T(8,128)(2,1)S(1)} fusion(f32[4,8,128,128,6]{3,2,4,1,0:T(8,128)} %get-tuple-element.42, f32[128,4,6]{0,2,1:T(8,128)S(1)} %get-tuple-element.41, pred[8]{0:T(512)(128)(4,1)S(1)} %get-tuple-element.52, bf16[8,128,4,128]{1,3,2,0:T(8,128)(2,1)S(1)} %get-tuple-element.29, f32[128,4,6]{0,2,1:T(8,128)S(1)} %get-tuple-element.9), kind=kOutput, calls=%fused_computation.52 | convolution fusion | flops 818675712 | bytes 14442504 | tf_op jit(solution)/shard_map/qgrpk,pkgd->qgrd/dot_general | solution.py:39
  570.7 0.0 copy-start.7
  570.7 2.5 fusion.10
  573.2 3.3 fusion.26
  576.5 0.1 pad_maximum_fusion.4
  576.7 1.6 copy.60
  578.2 3.4 pad_maximum_fusion
  (18 shorter events, 0.1 us)
Async XLA Ops:
  34.6 413.0 %all-to-all-start = ((bf16[16,32,8,2048]{3,2,1,0:T(8,128)(2,1)}), bf16[16,32,8,2048]{3,2,1,0:T(8,128)(2,1)}, u32[]{:S(2)}, u32[]{:S(2)}) async-start(bf16[16,32,8,2048]{3,2,1,0:T(8,128)(2,1)} %stack.2), calls=%async_computation | async-start | bytes 33554432 | tf_op jit(solution)/shard_map/all_to_all | solution.py:56
  45.1 213.1 %all-gather.2.cloned.1.call-start = ((), (), s32[]{:S(2)}) async-start(), calls=%async_computation.2 | async-start | bytes 8912896 | tf_op jit(solution)/shard_map/all_gather | solution.py:58
  48.0 3.2 copy-start.9
  48.0 3.2 copy-start.10
  477.9 3.2 copy-start.1
  498.9 2.9 copy-start.2
  498.9 2.9 copy-start.4
  501.8 6.3 %copy-start.6 = (bf16[8,128,4,128]{3,1,0,2:T(8,128)(2,1)S(1)}, bf16[8,128,4,128]{3,1,0,2:T(8,128)(2,1)}, u32[]{:S(2)}) copy-start(bf16[8,128,4,128]{3,1,0,2:T(8,128)(2,1)} %copy.90) | copy-start | bytes 3145732
  523.1 2.6 copy-start.8
  547.8 1.8 copy-start.3
  549.6 6.3 %copy-start.5 = (bf16[8,128,4,128]{3,1,0,2:T(8,128)(2,1)S(1)}, bf16[8,128,4,128]{3,1,0,2:T(8,128)(2,1)}, u32[]{:S(2)}) copy-start(bf16[8,128,4,128]{3,1,0,2:T(8,128)(2,1)} %copy.97) | copy-start | bytes 3145732
  570.7 2.5 copy-start.7
  576.5 1.7 copy-start
Sparse Core Ops, SparseCore 0:
  47.8 210.3 all-gather.1
